TPU v7x, 32 devices: a whole 2x2x4 slice. The times are simulated.
32 devices in a mesh: shard: 2 (over core), ctx: 4 (over y, x), tensor: 4 (over z).
Axes of the slice: x: 2, y: 2, z: 4, core: 2. Of those that a mesh axis runs over, the one named last changes fastest.
Arguments:
- inputs: bfloat16 [2, 2048, 2048], P('shard', ('ctx', 'tensor')), may hold values from -6 to 6
- out_grad: bfloat16 [2, 2048, 2048], P('shard', ('ctx', 'tensor')), may hold values from -6 to 6
- block_order: int32 [2, 8], P('shard'), may hold values from 0 to 7, each once within a row
- gain_attn: bfloat16 [2048], P(('shard', 'ctx')), may hold values from 0.5 to 1.5
- w_query: bfloat16 [2048, 2048], P(('shard', 'ctx'), 'tensor'), may hold values from -0.125 to 0.125
- w_keyval: bfloat16 [2048, 512], P(('shard', 'ctx'), 'tensor'), may hold values from -0.125 to 0.125
- w_output: bfloat16 [2048, 2048], P(('shard', 'ctx'), 'tensor'), may hold values from -3 to 3
- gain_mlp: bfloat16 [2048], P(('shard', 'ctx')), may hold values from 0.5 to 1.5
- w_gate: bfloat16 [2048, 5632], P(('shard', 'ctx'), 'tensor'), may hold values from -0.125 to 0.125
- w_up: bfloat16 [2048, 5632], P(('shard', 'ctx'), 'tensor'), may hold values from -0.125 to 0.125
- w_down: bfloat16 [2048, 5632], P(('shard', 'ctx'), 'tensor'), may hold values from -0.078125 to 0.078125
Outputs:
- layer_out: bfloat16 [2, 2048, 2048], P('shard', ('ctx', 'tensor'))
- input_grad: float32 [2, 2048, 2048], P('shard', ('ctx', 'tensor'))
- grad_gain_attn: float32 [2048], P(('shard', 'ctx'))
- grad_query: float32 [2048, 2048], P(('shard', 'ctx'), 'tensor')
- grad_keyval: float32 [2048, 512], P(('shard', 'ctx'), 'tensor')
- grad_output: float32 [2048, 2048], P(('shard', 'ctx'), 'tensor')
- grad_gain_mlp: float32 [2048], P(('shard', 'ctx'))
- grad_gate: float32 [2048, 5632], P(('shard', 'ctx'), 'tensor')
- grad_up: float32 [2048, 5632], P(('shard', 'ctx'), 'tensor')
- grad_down: float32 [2048, 5632], P(('shard', 'ctx'), 'tensor')
Inputs may be any that keep to these rules, and one draw needn't show every extreme that they name: `block_order`: each row is a permutation of the blocks of one sequence.
All inputs are finite; a program needn't handle non-finite values.
Results may differ from a plain program's by a relative error of at most 0.014.
Values may be sent and summed in bfloat16 or wider, within the bound.
A program may use at most 192 MiB of HBM per device.

v0:
```python
import jax
import jax.numpy as jnp
from jax import lax
from jax.sharding import PartitionSpec as P

HD = 64
BLOCK = 256
BLOCKS = 8
epsilon = 1e-05
blocked = -1e30


def apply_norm(values_in):
    inverse_root_mean = lax.rsqrt(jnp.mean(values_in * values_in, -1, keepdims=True) + epsilon)
    return (values_in * inverse_root_mean, inverse_root_mean)


def norm_backward_pass(normed_gradient, unit_rows, inverse_root_mean, norm_scale):
    unit_rows_gradient = normed_gradient * norm_scale
    scale_gradient = jnp.sum(normed_gradient * unit_rows, axis=(0, 1))
    value_gradients = inverse_root_mean * (
        unit_rows_gradient - unit_rows * jnp.mean(unit_rows_gradient * unit_rows, -1, keepdims=True)
    )
    return (scale_gradient, value_gradients)


def rotary_tables(position, width):
    half_width = width // 2
    frequency = 10000.0 ** (-jnp.arange(half_width, dtype=jnp.float32) * 2.0 / width)
    angles = position.astype(jnp.float32)[..., None] * frequency
    return (jnp.cos(angles)[:, :, None, :], jnp.sin(angles)[:, :, None, :])


def rotate(values_in, cosine_table, sine_table):
    half_width = values_in.shape[-1] // 2
    first_half = values_in[..., :half_width]
    second = values_in[..., half_width:]
    return jnp.concatenate(
        [
            first_half * cosine_table - second * sine_table,
            second * cosine_table + first_half * sine_table,
        ],
        -1,
    )


def unrotate(grad_in, cosine_table, sine_table):
    half_width = grad_in.shape[-1] // 2
    first_half = grad_in[..., :half_width]
    second = grad_in[..., half_width:]
    return jnp.concatenate(
        [
            first_half * cosine_table + second * sine_table,
            second * cosine_table - first_half * sine_table,
        ],
        -1,
    )


def broadcast_rows(values_in):
    return lax.all_gather(values_in, "tensor", axis=1, tiled=True)


def spread_grads(values_in):
    return lax.all_gather(values_in, "tensor", axis=1, tiled=True)


def branch_sum(partial_sum):
    return lax.psum_scatter(partial_sum, "tensor", scatter_dimension=1, tiled=True)


def input_sum(partial_sum):
    return lax.psum_scatter(partial_sum, "tensor", scatter_dimension=1, tiled=True)


def body(
    inputs,
    out_grad,
    block_order,
    gain_attn,
    w_query,
    w_keyval,
    w_output,
    gain_mlp,
    w_gate,
    w_up,
    w_down,
):
    seq_count = inputs.shape[0]
    length = BLOCK * BLOCKS
    query_rows = length // lax.axis_size("ctx")
    heads_here = w_query.shape[1] // HD
    groups_here = w_keyval.shape[1] // (2 * HD)
    per_group = heads_here // groups_here
    inv_root = HD ** (-0.5)
    f32 = jnp.float32
    brain_float_sixteen = jnp.bfloat16
    slot_index = jnp.arange(length, dtype=jnp.int32)
    chooser = (slot_index // BLOCK)[:, None] == jnp.arange(BLOCKS, dtype=jnp.int32)[None, :]
    block_all = jnp.sum(jnp.where(chooser[None, :, :], block_order[:, None, :], 0), axis=-1)
    position_all = block_all * BLOCK + slot_index % BLOCK
    row_start = lax.axis_index("ctx") * query_rows
    block_here = lax.dynamic_slice_in_dim(block_all, row_start, query_rows, 1)
    position_here = lax.dynamic_slice_in_dim(position_all, row_start, query_rows, 1)
    allowed = block_all[:, None, :] <= block_here[:, :, None]
    cosine_table, sine_table = rotary_tables(position_here, HD)
    group_ids = jnp.arange(heads_here, dtype=jnp.int32) // per_group
    attention_norm_scale, query_all, keyval_all, output_all = (
        lax.all_gather(gain_attn, ("shard", "ctx"), axis=0, tiled=True),
        lax.all_gather(w_query, ("shard", "ctx"), axis=0, tiled=True),
        lax.all_gather(w_keyval, ("shard", "ctx"), axis=0, tiled=True),
        lax.all_gather(w_output, ("shard", "ctx"), axis=0, tiled=True),
    )
    feedforward_norm_scale, gate_all, up_all, down_all = (
        lax.all_gather(gain_mlp, ("shard", "ctx"), axis=0, tiled=True),
        lax.all_gather(w_gate, ("shard", "ctx"), axis=0, tiled=True),
        lax.all_gather(w_up, ("shard", "ctx"), axis=0, tiled=True),
        lax.all_gather(w_down, ("shard", "ctx"), axis=0, tiled=True),
    )
    attention_norm_scale = attention_norm_scale.astype(f32)
    feedforward_norm_scale = feedforward_norm_scale.astype(f32)
    residual_stream = inputs.astype(f32)
    first_unit_rows, first_inverse_root = apply_norm(residual_stream)
    first_normed = broadcast_rows(
        (first_unit_rows * attention_norm_scale).astype(brain_float_sixteen)
    )
    query_raw = jnp.einsum("sqd,dh->sqh", first_normed, query_all, preferred_element_type=f32)
    keyval_raw = jnp.einsum("sqd,dh->sqh", first_normed, keyval_all, preferred_element_type=f32)
    query_raw = query_raw.reshape(seq_count, query_rows, heads_here, HD)
    keyval_raw = keyval_raw.reshape(seq_count, query_rows, groups_here, 2 * HD)
    queries = rotate(query_raw, cosine_table, sine_table).astype(brain_float_sixteen)
    keys_here = rotate(keyval_raw[..., :HD], cosine_table, sine_table).astype(brain_float_sixteen)
    values_here = keyval_raw[..., HD:].astype(brain_float_sixteen)
    keyval_here = jnp.concatenate([keys_here, values_here], -1).reshape(
        seq_count, query_rows, groups_here * 2 * HD
    )
    keyval_seq = lax.all_gather(keyval_here, "ctx", axis=1, tiled=True).reshape(
        seq_count, length, groups_here, 2 * HD
    )
    query_heads = jnp.moveaxis(queries, 2, 0)

    def scores_of(query_head, group_id):
        keyval_group = lax.dynamic_index_in_dim(keyval_seq, group_id, 2, keepdims=False)
        keys_group = keyval_group[..., :HD]
        values_group = keyval_group[..., HD:]
        raw_scores = (
            jnp.einsum("sqd,skd->sqk", query_head, keys_group, preferred_element_type=f32)
            * inv_root
        )
        return (jnp.where(allowed, raw_scores, blocked), keys_group, values_group)

    def forward_head(operands):
        query_head, group_id = operands
        masked, keys_group, values_group = scores_of(query_head, group_id)
        row_max = jnp.max(masked, -1, keepdims=True)
        exponent = jnp.exp(masked - row_max)
        expsum = jnp.sum(exponent, -1, keepdims=True)
        weights = (exponent / expsum).astype(brain_float_sixteen)
        head_out = jnp.einsum(
            "sqk,skd->sqd", weights, values_group, preferred_element_type=f32
        ).astype(brain_float_sixteen)
        return (head_out, (row_max + jnp.log(expsum))[..., 0])

    head_outs, log_sums = lax.map(forward_head, (query_heads, group_ids))
    attn_out = jnp.moveaxis(head_outs, 0, 2).reshape(seq_count, query_rows, heads_here * HD)
    attn_branch = branch_sum(
        jnp.einsum("sqh,dh->sqd", attn_out, output_all, preferred_element_type=f32)
    )
    between_rows = residual_stream + attn_branch
    second_unit_rows, second_inverse_root = apply_norm(between_rows)
    second_normed = broadcast_rows(
        (second_unit_rows * feedforward_norm_scale).astype(brain_float_sixteen)
    )
    gate_act = jnp.einsum("sqd,df->sqf", second_normed, gate_all, preferred_element_type=f32)
    up_act = jnp.einsum("sqd,df->sqf", second_normed, up_all, preferred_element_type=f32)
    sig_gate = jax.nn.sigmoid(gate_act)
    silu_gate = gate_act * sig_gate
    hidden = (silu_gate * up_act).astype(brain_float_sixteen)
    mlp_branch = branch_sum(jnp.einsum("sqf,df->sqd", hidden, down_all, preferred_element_type=f32))
    layer_out = (between_rows + mlp_branch).astype(brain_float_sixteen)
    attention_norm_scale, query_all, keyval_all, output_all = (
        lax.all_gather(gain_attn, ("shard", "ctx"), axis=0, tiled=True),
        lax.all_gather(w_query, ("shard", "ctx"), axis=0, tiled=True),
        lax.all_gather(w_keyval, ("shard", "ctx"), axis=0, tiled=True),
        lax.all_gather(w_output, ("shard", "ctx"), axis=0, tiled=True),
    )
    feedforward_norm_scale, gate_all, up_all, down_all = (
        lax.all_gather(gain_mlp, ("shard", "ctx"), axis=0, tiled=True),
        lax.all_gather(w_gate, ("shard", "ctx"), axis=0, tiled=True),
        lax.all_gather(w_up, ("shard", "ctx"), axis=0, tiled=True),
        lax.all_gather(w_down, ("shard", "ctx"), axis=0, tiled=True),
    )
    attention_norm_scale = attention_norm_scale.astype(f32)
    feedforward_norm_scale = feedforward_norm_scale.astype(f32)
    grad_mlp_rows = spread_grads(out_grad)
    d_hidden = jnp.einsum("sqd,df->sqf", grad_mlp_rows, down_all, preferred_element_type=f32)
    grad_down_w = jnp.einsum("sqd,sqf->df", grad_mlp_rows, hidden, preferred_element_type=f32)
    d_gate = (d_hidden * up_act * sig_gate * (1.0 + gate_act * (1.0 - sig_gate))).astype(
        brain_float_sixteen
    )
    d_up = (d_hidden * silu_gate).astype(brain_float_sixteen)
    grad_gate_w = jnp.einsum("sqd,sqf->df", second_normed, d_gate, preferred_element_type=f32)
    grad_up_w = jnp.einsum("sqd,sqf->df", second_normed, d_up, preferred_element_type=f32)
    second_normed_gradient = input_sum(
        jnp.einsum("sqf,df->sqd", d_gate, gate_all, preferred_element_type=f32)
        + jnp.einsum("sqf,df->sqd", d_up, up_all, preferred_element_type=f32)
    )
    feedforward_scale_gradient, middle_gradient = norm_backward_pass(
        second_normed_gradient, second_unit_rows, second_inverse_root, feedforward_norm_scale
    )
    middle_gradient = middle_gradient + out_grad.astype(f32)
    grad_attn_rows = spread_grads(middle_gradient.astype(brain_float_sixteen))
    d_attn = jnp.einsum(
        "sqd,dh->sqh", grad_attn_rows, output_all, preferred_element_type=f32
    ).astype(brain_float_sixteen)
    grad_output_w = jnp.einsum("sqd,sqh->dh", grad_attn_rows, attn_out, preferred_element_type=f32)
    d_heads = jnp.moveaxis(d_attn.reshape(seq_count, query_rows, heads_here, HD), 2, 0)

    def backward_head(accumulated, operands):
        query_head, d_head, log_sum, group_id = operands
        masked, keys_group, values_group = scores_of(query_head, group_id)
        probs_f = jnp.exp(masked - log_sum[..., None])
        d_prob = jnp.einsum("sqd,skd->sqk", d_head, values_group, preferred_element_type=f32)
        row_delta = jnp.sum(probs_f * d_prob, -1, keepdims=True)
        d_score = (probs_f * (d_prob - row_delta)).astype(brain_float_sixteen)
        d_query = (
            jnp.einsum("sqk,skd->sqd", d_score, keys_group, preferred_element_type=f32) * inv_root
        )
        d_key = (
            jnp.einsum("sqk,sqd->skd", d_score, query_head, preferred_element_type=f32) * inv_root
        )
        d_value = jnp.einsum(
            "sqk,sqd->skd", probs_f.astype(brain_float_sixteen), d_head, preferred_element_type=f32
        )
        current = lax.dynamic_index_in_dim(accumulated, group_id, 2, keepdims=False)
        accumulated = lax.dynamic_update_index_in_dim(
            accumulated, current + jnp.concatenate([d_key, d_value], -1), group_id, 2
        )
        return (accumulated, d_query)

    zero_grads = jnp.zeros((seq_count, length, groups_here, 2 * HD), f32)
    d_keyval_seq, d_queries = lax.scan(
        backward_head, zero_grads, (query_heads, d_heads, log_sums, group_ids)
    )
    d_keyval = lax.psum_scatter(
        d_keyval_seq.reshape(seq_count, length, groups_here * 2 * HD),
        "ctx",
        scatter_dimension=1,
        tiled=True,
    ).reshape(seq_count, query_rows, groups_here, 2 * HD)
    d_keyval_raw = (
        jnp.concatenate(
            [unrotate(d_keyval[..., :HD], cosine_table, sine_table), d_keyval[..., HD:]], -1
        )
        .astype(brain_float_sixteen)
        .reshape(seq_count, query_rows, groups_here * 2 * HD)
    )
    d_query_raw = (
        unrotate(jnp.moveaxis(d_queries, 0, 2), cosine_table, sine_table)
        .astype(brain_float_sixteen)
        .reshape(seq_count, query_rows, heads_here * HD)
    )
    grad_query_w = jnp.einsum("sqd,sqh->dh", first_normed, d_query_raw, preferred_element_type=f32)
    grad_keyval_w = jnp.einsum(
        "sqd,sqh->dh", first_normed, d_keyval_raw, preferred_element_type=f32
    )
    first_normed_gradient = input_sum(
        jnp.einsum("sqh,dh->sqd", d_query_raw, query_all, preferred_element_type=f32)
        + jnp.einsum("sqh,dh->sqd", d_keyval_raw, keyval_all, preferred_element_type=f32)
    )
    attention_scale_gradient, residual_gradient = norm_backward_pass(
        first_normed_gradient, first_unit_rows, first_inverse_root, attention_norm_scale
    )
    input_grad = middle_gradient + residual_gradient
    gain_a_sum, grad_query, grad_keyval, grad_output = (
        lax.psum_scatter(
            attention_scale_gradient, ("shard", "ctx"), scatter_dimension=0, tiled=True
        ),
        lax.psum_scatter(grad_query_w, ("shard", "ctx"), scatter_dimension=0, tiled=True),
        lax.psum_scatter(grad_keyval_w, ("shard", "ctx"), scatter_dimension=0, tiled=True),
        lax.psum_scatter(grad_output_w, ("shard", "ctx"), scatter_dimension=0, tiled=True),
    )
    gain_m_sum, grad_gate, grad_up, grad_down = (
        lax.psum_scatter(
            feedforward_scale_gradient, ("shard", "ctx"), scatter_dimension=0, tiled=True
        ),
        lax.psum_scatter(grad_gate_w, ("shard", "ctx"), scatter_dimension=0, tiled=True),
        lax.psum_scatter(grad_up_w, ("shard", "ctx"), scatter_dimension=0, tiled=True),
        lax.psum_scatter(grad_down_w, ("shard", "ctx"), scatter_dimension=0, tiled=True),
    )
    grad_gain_attn, grad_gain_mlp = lax.psum((gain_a_sum, gain_m_sum), "tensor")
    return (
        layer_out,
        input_grad,
        grad_gain_attn,
        grad_query,
        grad_keyval,
        grad_output,
        grad_gain_mlp,
        grad_gate,
        grad_up,
        grad_down,
    )


def solution(mesh):
    return jax.shard_map(
        body,
        mesh=mesh,
        in_specs=(
            P("shard", ("ctx", "tensor"), None),
            P("shard", ("ctx", "tensor"), None),
            P("shard", None),
            P(("shard", "ctx")),
            P(("shard", "ctx"), "tensor"),
            P(("shard", "ctx"), "tensor"),
            P(("shard", "ctx"), "tensor"),
            P(("shard", "ctx")),
            P(("shard", "ctx"), "tensor"),
            P(("shard", "ctx"), "tensor"),
            P(("shard", "ctx"), "tensor"),
        ),
        out_specs=(
            P("shard", ("ctx", "tensor"), None),
            P("shard", ("ctx", "tensor"), None),
            P(("shard", "ctx")),
            P(("shard", "ctx"), "tensor"),
            P(("shard", "ctx"), "tensor"),
            P(("shard", "ctx"), "tensor"),
            P(("shard", "ctx")),
            P(("shard", "ctx"), "tensor"),
            P(("shard", "ctx"), "tensor"),
            P(("shard", "ctx"), "tensor"),
        ),
        check_vma=False,
    )
```

profile of v0, /device:TPU:0, one launch (start us, length us, event | category | flops | bytes accessed | tf_op | source)
XLA Modules:
  0.0 1319.3 jit_solution(5621312489691871391)
XLA Ops:
  7.9 14.8 %all-gather.1 = bf16[8,1,256]{2,1,0:T(2,128)(2,1)S(1)} all-gather(bf16[1,1,256]{2,1,0:T(2,128)(2,1)S(1)} %reshape.754), channel_id=1, replica_groups=mesh['shard'=2,'ctx'=4,'tensor'=4] {'shard','ctx'}, dimensions={0}, use_global_device_ids=true | all-gather | bytes 4608 | tf_op jit(solution)/shard_map/all_gather | solution.py:109
  29.0 26.2 %all_gather.50 = bf16[2048,128]{1,0:T(8,128)(2,1)S(1)} all-gather(bf16[256,128]{1,0:T(8,128)(2,1)} %param.20), channel_id=1, replica_groups=mesh['shard'=2,'ctx'=4,'tensor'=4] {'shard','ctx'}, dimensions={0}, use_global_device_ids=true | all-gather | bytes 589824 | tf_op jit(solution)/shard_map/all_gather | solution.py:111
  55.5 18.2 %all-gather.13.cloned.1.call-done = bf16[1,512,2048]{2,1,0:T(8,128)(2,1)} async-done(((bf16[1,128,2048]{2,1,0:T(8,128)(2,1)}), bf16[1,512,2048]{2,1,0:T(8,128)(2,1)}) %all-gather.13.cloned.1.call-update) | async-done | bytes 2097168 | tf_op jit(solution)/shard_map/all_gather | solution.py:61
  76.5 12.3 all-gather
  89.2 13.1 all-gather.15.cloned.1.call-done
  102.3 3.9 copy.45
  106.2 2.9 fusion.57
  110.7 29.5 %while.28 = (s32[]{:T(128)}, bf16[8,1,512,64]{2,3,1,0:T(8,128)(2,1)S(1)}, f32[8,1,512]{2,1,0:T(1,128)S(1)}, bf16[8,1,512,64]{3,2,1,0:T(8,128)(2,1)}, bf16[1,2048...) while((s32[]{:T(128)}, ...), condition=%wide.region_5.6_spmd.clone, body=%wide.region_2.5_spmd.clone.sunk | while | flops 277904896 | bytes 13859421 | solution.py:164
  140.3 5.1 convolution_bitcast_fusion.3
  146.0 13.7 %all-gather.2 = bf16[8,1,256]{2,1,0:T(2,128)(2,1)S(1)} all-gather(bf16[1,1,256]{2,1,0:T(2,128)(2,1)S(1)} %reshape.756), channel_id=1, replica_groups=mesh['shard'=2,'ctx'=4,'tensor'=4] {'shard','ctx'}, dimensions={0}, use_global_device_ids=true | all-gather | bytes 4608 | tf_op jit(solution)/shard_map/all_gather | solution.py:115
  159.8 62.6 %reduce-scatter.12.cloned.1.call-done = f32[1,128,2048]{2,1,0:T(8,128)} async-done(((f32[1,512,2048]{2,1,0:T(8,128)}), f32[1,128,2048]{2,1,0:T(8,128)}) %reduce-scatter.12.cloned.1.call-update) | async-done | bytes 1048592 | tf_op jit(solution)/shard_map/reduce_scatter | solution.py:69
  227.7 40.3 %all-gather.23.cloned.1.call-done = bf16[2048,1408]{1,0:T(8,128)(2,1)} async-done(((bf16[256,1408]{1,0:T(8,128)(2,1)}), bf16[2048,1408]{1,0:T(8,128)(2,1)}) %all-gather.23.cloned.1.call-update) | async-done | bytes 5767184 | tf_op jit(solution)/shard_map/all_gather | solution.py:117
  268.1 48.0 %all-gather.19.cloned.1.call-done = bf16[1,512,2048]{2,1,0:T(8,128)(2,1)} async-done(((bf16[1,128,2048]{2,1,0:T(8,128)(2,1)}), bf16[1,512,2048]{2,1,0:T(8,128)(2,1)}) %all-gather.19.cloned.1.call-update) | async-done | bytes 2097168 | tf_op jit(solution)/shard_map/all_gather | solution.py:61
  316.1 8.3 fusion.41
  324.4 35.8 %all-gather.21.cloned.1.call-done = bf16[2048,1408]{1,0:T(8,128)(2,1)} async-done(((bf16[256,1408]{1,0:T(8,128)(2,1)}), bf16[2048,1408]{1,0:T(8,128)(2,1)}) %all-gather.21.cloned.1.call-update) | async-done | bytes 5767184 | tf_op jit(solution)/shard_map/all_gather | solution.py:116
  360.2 8.2 fusion.43
  368.4 39.4 %all-gather.27.cloned.1.call-done = bf16[1,512,2048]{2,1,0:T(8,128)(2,1)} async-done(((bf16[1,128,2048]{2,1,0:T(8,128)(2,1)}), bf16[1,512,2048]{2,1,0:T(8,128)(2,1)}) %all-gather.27.cloned.1.call-update) | async-done | bytes 2097168 | tf_op jit(solution)/shard_map/all_gather | solution.py:65
  407.8 44.1 %all-gather.25.cloned.1.call-done = bf16[2048,1408]{1,0:T(8,128)(2,1)} async-done(((bf16[256,1408]{1,0:T(8,128)(2,1)}), bf16[2048,1408]{1,0:T(8,128)(2,1)}) %all-gather.25.cloned.1.call-update) | async-done | bytes 5767184 | tf_op jit(solution)/shard_map/all_gather | solution.py:118
  451.9 10.4 multiply_convert_fusion.1
  462.4 3.4 fusion.101
  465.8 7.7 add_bitcast_fusion.1
  473.6 76.9 %reduce-scatter.16.cloned.1.call-done = f32[1,128,2048]{2,1,0:T(8,128)} async-done(((f32[1,512,2048]{2,1,0:T(8,128)}), f32[1,128,2048]{2,1,0:T(8,128)}) %reduce-scatter.16.cloned.1.call-update) | async-done | bytes 1048592 | tf_op jit(solution)/shard_map/reduce_scatter | solution.py:73
  554.7 46.4 %all-gather.29.cloned.1.call-done = bf16[1,512,2048]{2,1,0:T(8,128)(2,1)} async-done(((bf16[1,128,2048]{2,1,0:T(8,128)(2,1)}), bf16[1,512,2048]{2,1,0:T(8,128)(2,1)}) %all-gather.29.cloned.1.call-update) | async-done | bytes 2097168 | tf_op jit(solution)/shard_map/all_gather | solution.py:65
  601.1 3.5 fusion.60
  605.9 96.6 %while.29 = (s32[]{:T(128)}, f32[1,2048,1,128]{1,3,2,0:T(8,128)}, f32[8,1,512,64]{2,3,1,0:T(8,128)}, bf16[8,1,512,64]{3,2,1,0:T(8,128)(2,1)}, bf16[1,2048,1,128]...) while((s32[]{:T(128)}, f32[1,2048,1,128]{1,3,2,0:T(8,128)}, ...), condition=%wide.region_13.14_spmd.clone, body=%wide.region_11.13_spmd.clone.sunk | while | flops 682524160 | bytes 37902968 | solution.py:242
  625.9 2.5 maximum_add_fusion.2
  650.2 2.5 maximum_add_fusion.2
  702.7 9.5 convolution_bitcast_fusion.1
  714.2 3.2 fusion.102
  717.5 11.7 reduce-scatter.18.cloned.1.call-done
  731.3 4.8 add_bitcast_fusion
  737.5 8.5 convolution_bitcast_fusion.2
  750.0 9.9 fusion.39
  760.0 10.4 fusion.37
  771.4 5.2 fusion.30
  776.9 3.4 fusion.47
  782.2 37.7 %reduce-scatter.32.cloned.1.call-done = f32[256,1408]{0,1:T(8,128)} async-done(((f32[2048,1408]{0,1:T(8,128)}), f32[256,1408]{0,1:T(8,128)}) %reduce-scatter.32.cloned.1.call-update) | async-done | bytes 1441808 | tf_op jit(solution)/shard_map/reduce_scatter | solution.py:289
  819.9 2.9 copy.52
  822.8 76.1 %reduce-scatter.20.cloned.1.call-done = f32[1,128,2048]{2,1,0:T(8,128)} async-done(((f32[1,512,2048]{2,1,0:T(8,128)}), f32[1,128,2048]{2,1,0:T(8,128)}) %reduce-scatter.20.cloned.1.call-update) | async-done | bytes 1048592 | tf_op jit(solution)/shard_map/reduce_scatter | solution.py:73
  900.5 26.9 %all-reduce.2 = (f32[2048]{0:T(1024)S(1)}, f32[2048]{0:T(1024)S(1)}) all-reduce(f32[2048]{0:T(1024)S(1)} %get-tuple-element.284, f32[2048]{0:T(1024)S(1)} %get-tuple-element.282), channel_id=8, replica_groups=mesh['shard'=2,'ctx'=4,'tensor'=4] {'shard','ctx'}, use_global_device_ids=true, to_apply=%region_18.19.clone | all-reduce | flops 4096 | bytes 32768
  927.6 12.4 all-reduce.3
  939.9 38.7 %reduce-scatter.14.cloned.1.call-done = f32[1,128,2048]{2,1,0:T(8,128)} async-done(((f32[1,512,2048]{2,1,0:T(8,128)}), f32[1,128,2048]{2,1,0:T(8,128)}) %reduce-scatter.14.cloned.1.call-update) | async-done | bytes 1048592 | tf_op jit(solution)/shard_map/reduce_scatter | solution.py:69
  978.7 3.2 fusion.70
  981.8 37.3 %reduce-scatter.24.cloned.1.call-done = f32[256,128]{1,0:T(8,128)} async-done(((f32[2048,128]{1,0:T(8,128)}), f32[256,128]{1,0:T(8,128)}) %reduce-scatter.24.cloned.1.call-update) | async-done | bytes 131088 | tf_op jit(solution)/shard_map/reduce_scatter | solution.py:280
  1019.1 91.1 %reduce-scatter.28.cloned.1.call-done = f32[256,1408]{1,0:T(8,128)} async-done(((f32[2048,1408]{1,0:T(8,128)}), f32[256,1408]{1,0:T(8,128)}) %reduce-scatter.28.cloned.1.call-update) | async-done | bytes 1441808 | tf_op jit(solution)/shard_map/reduce_scatter | solution.py:287
  1110.3 91.1 %reduce-scatter.30.cloned.1.call-done = f32[256,1408]{1,0:T(8,128)} async-done(((f32[2048,1408]{1,0:T(8,128)}), f32[256,1408]{1,0:T(8,128)}) %reduce-scatter.30.cloned.1.call-update) | async-done | bytes 1441808 | tf_op jit(solution)/shard_map/reduce_scatter | solution.py:288
  1201.4 55.6 %reduce-scatter.26.cloned.1.call-done = f32[256,512]{1,0:T(8,128)} async-done(((f32[2048,512]{1,0:T(8,128)}), f32[256,512]{1,0:T(8,128)}) %reduce-scatter.26.cloned.1.call-update) | async-done | bytes 524304 | tf_op jit(solution)/shard_map/reduce_scatter | solution.py:281
  1257.0 55.1 %reduce-scatter.22.cloned.1.call-done = f32[256,512]{1,0:T(8,128)} async-done(((f32[2048,512]{1,0:T(8,128)}), f32[256,512]{1,0:T(8,128)}) %reduce-scatter.22.cloned.1.call-update) | async-done | bytes 524304 | tf_op jit(solution)/shard_map/reduce_scatter | solution.py:279
  (244 shorter events, 158.0 us)
Async XLA Ops:
  7.2 66.6 %all-gather.13.cloned.1.call-start = ((), (), s32[]{:S(2)}) async-start(), calls=%async_computation.11 | async-start | bytes 2621440 | tf_op jit(solution)/shard_map/all_gather | solution.py:61
  22.7 1.3 copy-start.15
  26.5 75.8 %all-gather.15.cloned.1.call-start = ((), (), s32[]{:S(2)}) async-start(), calls=%async_computation.12 | async-start | bytes 2359296 | tf_op jit(solution)/shard_map/all_gather | solution.py:110
  27.3 113.0 %all-gather.17.cloned.1.call-start = ((), (), s32[]{:S(2)}) async-start(), calls=%async_computation.13 | async-start | bytes 2359296 | tf_op jit(solution)/shard_map/all_gather | solution.py:112
  28.0 194.3 %reduce-scatter.12.cloned.1.call-start = ((), (), s32[]{:S(2)}) async-start(), calls=%async_computation.14 | async-start | bytes 5242880 | tf_op jit(solution)/shard_map/reduce_scatter | solution.py:69
  28.1 61.1 %copy-start.21 = (f32[32]{0:T(128)}, f32[32]{0:T(128)S(1)}, u32[]{:S(2)}) copy-start(f32[32]{0:T(128)S(1)} %multiply_power_fusion) | copy-start | bytes 388
  29.0 60.2 %copy-start.17 = (f32[1,512]{1,0:T(1,128)}, f32[1,512]{1,0:T(1,128)S(1)}, u32[]{:S(2)}) copy-start(f32[1,512]{1,0:T(1,128)S(1)} %fusion.96) | copy-start | bytes 6148
  55.2 21.3 %copy-start.10 = (bf16[2048,128]{1,0:T(8,128)(2,1)}, bf16[2048,128]{1,0:T(8,128)(2,1)S(1)}, u32[]{:S(2)}) copy-start(bf16[2048,128]{1,0:T(8,128)(2,1)S(1)} %all_gather.50) | copy-start | bytes 1572868
  76.5 29.7 %copy-start = (bf16[1,512,2048]{2,1,0:T(8,128)(2,1)S(1)}, bf16[1,512,2048]{2,1,0:T(8,128)(2,1)}, u32[]{:S(2)}) copy-start(bf16[1,512,2048]{2,1,0:T(8,128)(2,1)} %all-gather.13.cloned.1.call-done) | copy-start | bytes 6291460
  109.1 1.6 copy-start.12
  140.2 5.1 copy-start.13
  145.3 0.7 copy-start.24
  145.4 77.0 %copy-start.4 = (bf16[1,128,2048]{2,1,0:T(8,128)(2,1)S(1)}, bf16[1,128,2048]{2,1,0:T(8,128)(2,1)}, u32[]{:S(2)}) copy-start(bf16[1,128,2048]{2,1,0:T(8,128)(2,1)} %param.15) | copy-start | bytes 1572868
  145.4 122.7 %all-gather.23.cloned.1.call-start = ((), (), s32[]{:S(2)}) async-start(), calls=%async_computation.17 | async-start | bytes 6488064 | tf_op jit(solution)/shard_map/all_gather | solution.py:117
  146.0 170.1 %all-gather.19.cloned.1.call-start = ((), (), s32[]{:S(2)}) async-start(), calls=%async_computation.15 | async-start | bytes 2621440 | tf_op jit(solution)/shard_map/all_gather | solution.py:61
  223.8 328.3 %copy-start.2 = (f32[1,128,2048]{2,1,0:T(8,128)}, f32[1,128,2048]{2,1,0:T(8,128)S(1)}, u32[]{:S(2)}) copy-start(f32[1,128,2048]{2,1,0:T(8,128)S(1)} %get-tuple-element.323) | copy-start | bytes 3145732
  224.9 135.3 %all-gather.21.cloned.1.call-start = ((), (), s32[]{:S(2)}) async-start(), calls=%async_computation.16 | async-start | bytes 6488064 | tf_op jit(solution)/shard_map/all_gather | solution.py:116
  225.7 182.2 %all-gather.27.cloned.1.call-start = ((), (), s32[]{:S(2)}) async-start(), calls=%async_computation.20 | async-start | bytes 2621440 | tf_op jit(solution)/shard_map/all_gather | solution.py:65
  226.4 225.5 %all-gather.25.cloned.1.call-start = ((), (), s32[]{:S(2)}) async-start(), calls=%async_computation.18 | async-start | bytes 6488064 | tf_op jit(solution)/shard_map/all_gather | solution.py:118
  227.1 323.3 %reduce-scatter.16.cloned.1.call-start = ((), (), s32[]{:S(2)}) async-start(), calls=%async_computation.21 | async-start | bytes 5242880 | tf_op jit(solution)/shard_map/reduce_scatter | solution.py:73
  451.9 10.4 copy-start.23
  462.4 3.5 copy-start.28
  462.4 3.5 copy-start.27
  473.5 78.5 %copy-start.8 = (bf16[1,128,2048]{2,1,0:T(8,128)(2,1)S(1)}, bf16[1,128,2048]{2,1,0:T(8,128)(2,1)}, u32[]{:S(2)}) copy-start(bf16[1,128,2048]{2,1,0:T(8,128)(2,1)} %param.16) | copy-start | bytes 1572868
  473.5 127.5 %all-gather.29.cloned.1.call-start = ((), (), s32[]{:S(2)}) async-start(), calls=%async_computation.22 | async-start | bytes 2621440 | tf_op jit(solution)/shard_map/all_gather | solution.py:65
  554.4 174.8 %reduce-scatter.18.cloned.1.call-start = ((), (), s32[]{:S(2)}) async-start(), calls=%async_computation.23 | async-start | bytes 1310720 | tf_op jit(solution)/shard_map/reduce_scatter | solution.py:245
  702.6 117.3 %reduce-scatter.32.cloned.1.call-start = ((), (), s32[]{:S(2)}) async-start(), calls=%async_computation.30 | async-start | bytes 12976128 | tf_op jit(solution)/shard_map/reduce_scatter | solution.py:289
  712.2 2.0 copy-start.7
  712.2 186.7 %reduce-scatter.20.cloned.1.call-start = ((), (), s32[]{:S(2)}) async-start(), calls=%async_computation.24 | async-start | bytes 5242880 | tf_op jit(solution)/shard_map/reduce_scatter | solution.py:73
  714.2 15.0 %copy-start.18 = (f32[1,512]{1,0:T(1,128)S(1)}, f32[1,512]{1,0:T(1,128)}, u32[]{:S(2)}) copy-start(f32[1,512]{1,0:T(1,128)} %copy-done.17) | copy-start | bytes 6148
  714.2 15.0 %copy-start.22 = (f32[32]{0:T(128)S(1)}, f32[32]{0:T(128)}, u32[]{:S(2)}) copy-start(f32[32]{0:T(128)} %copy-done.21) | copy-start | bytes 388
  714.2 17.1 %copy-start.11 = (bf16[2048,128]{1,0:T(8,128)(2,1)S(1)}, bf16[2048,128]{1,0:T(8,128)(2,1)}, u32[]{:S(2)}) copy-start(bf16[2048,128]{1,0:T(8,128)(2,1)} %copy-done.10) | copy-start | bytes 1572868
  736.2 1.4 copy-start.26
  736.2 242.5 %reduce-scatter.14.cloned.1.call-start = ((), (), s32[]{:S(2)}) async-start(), calls=%async_computation.19 | async-start | bytes 5242880 | tf_op jit(solution)/shard_map/reduce_scatter | solution.py:69
  746.0 2.2 copy-start.1
  746.1 273.0 %reduce-scatter.24.cloned.1.call-start = ((), (), s32[]{:S(2)}) async-start(), calls=%async_computation.26 | async-start | bytes 1179648 | tf_op jit(solution)/shard_map/reduce_scatter | solution.py:280
  750.0 360.3 %reduce-scatter.28.cloned.1.call-start = ((), (), s32[]{:S(2)}) async-start(), calls=%async_computation.28 | async-start | bytes 12976128 | tf_op jit(solution)/shard_map/reduce_scatter | solution.py:287
  759.9 441.4 %reduce-scatter.30.cloned.1.call-start = ((), (), s32[]{:S(2)}) async-start(), calls=%async_computation.29 | async-start | bytes 12976128 | tf_op jit(solution)/shard_map/reduce_scatter | solution.py:288
  770.4 1.0 copy-start.14
  770.4 486.6 %reduce-scatter.26.cloned.1.call-start = ((), (), s32[]{:S(2)}) async-start(), calls=%async_computation.27 | async-start | bytes 4718592 | tf_op jit(solution)/shard_map/reduce_scatter | solution.py:281
  776.6 535.5 %reduce-scatter.22.cloned.1.call-start = ((), (), s32[]{:S(2)}) async-start(), calls=%async_computation.25 | async-start | bytes 4718592 | tf_op jit(solution)/shard_map/reduce_scatter | solution.py:279
  780.3 0.7 copy-start.25
  780.3 118.6 %copy-start.5 = (bf16[1,128,2048]{2,1,0:T(8,128)(2,1)S(1)}, bf16[1,128,2048]{2,1,0:T(8,128)(2,1)}, u32[]{:S(2)}) copy-start(bf16[1,128,2048]{2,1,0:T(8,128)(2,1)} %param.15) | copy-start | bytes 1572868
  780.3 118.6 %copy-start.16 = (f32[8,1,256]{2,1,0:T(1,128)S(1)}, f32[8,1,256]{2,1,0:T(1,128)}, u32[]{:S(2)}) copy-start(f32[8,1,256]{2,1,0:T(1,128)} %copy-done.15) | copy-start | bytes 24580
  780.3 118.6 %copy-start.20 = (f32[128]{0:T(128)S(1)}, f32[128]{0:T(128)}, u32[]{:S(2)}) copy-start(f32[128]{0:T(128)} %copy-done.19) | copy-start | bytes 1540
  780.4 198.3 %copy-start.3 = (f32[1,128,2048]{2,1,0:T(8,128)S(1)}, f32[1,128,2048]{2,1,0:T(8,128)}, u32[]{:S(2)}) copy-start(f32[1,128,2048]{2,1,0:T(8,128)} %copy-done.2) | copy-start | bytes 3145732
  780.4 198.3 %copy-start.6 = (f32[1,128,2048]{2,1,0:T(8,128)S(1)}, f32[1,128,2048]{2,1,0:T(8,128)}, u32[]{:S(2)}) copy-start(f32[1,128,2048]{2,1,0:T(8,128)} %reduce-scatter.16.cloned.1.call-done) | copy-start | bytes 3145732
  780.4 198.3 %copy-start.9 = (bf16[1,128,2048]{2,1,0:T(8,128)(2,1)S(1)}, bf16[1,128,2048]{2,1,0:T(8,128)(2,1)}, u32[]{:S(2)}) copy-start(bf16[1,128,2048]{2,1,0:T(8,128)(2,1)} %param.16) | copy-start | bytes 1572868
  (1 other events, 0.5 us)
Sparse Core Ops, SparseCore 0:
  26.6 47.0 all-gather.12
  75.6 26.6 all-gather.14
  104.2 27.8 all-gather.16
  145.5 76.7 reduce-scatter.11
  224.2 43.8 all-gather.22
  270.1 45.9 all-gather.18
  318.1 42.0 all-gather.20
  361.9 45.9 all-gather.26
  409.9 42.0 all-gather.24
  473.7 76.7 reduce-scatter.15
  554.6 46.4 all-gather.28
  702.7 26.4 reduce-scatter.17
  733.1 86.7 reduce-scatter.31
  822.2 76.7 reduce-scatter.19
  901.1 77.5 reduce-scatter.13
  982.6 36.4 reduce-scatter.23
  1023.4 86.7 reduce-scatter.27
  1114.6 86.7 reduce-scatter.29
  1205.7 51.2 reduce-scatter.25
  1260.8 51.3 reduce-scatter.21
where the time goes:
time: 1330 us; the launch traced here: 1320 us
  waiting for transfers between devices  924 us (69%)
  matrix products  206 us (15%)
  blocking collectives  106 us (8%)
  other arithmetic  47.6 us (4%)
  local copies, waits for them, and re-layouts  18.1 us (1%)
  between operations  15.7 us (1%)
    reduce_scatter x2, waiting for transfers between devices, input_sum(): lax.psum_scatter(partial_sum, 'tensor', scatter_dimension=1, tiled=True)  153 us
    reduce_scatter x2, waiting for transfers between devices, branch_sum(): lax.psum_scatter(partial_sum, 'tensor', scatter_dimension=1, tiled=True)  101 us
    reduce_scatter x1, waiting for transfers between devices, body(): lax.psum_scatter(grad_gate_w, ('shard', 'ctx'), scatter_dimension=0, tile...  91.1 us
    reduce_scatter x1, waiting for transfers between devices, body(): lax.psum_scatter(grad_up_w, ('shard', 'ctx'), scatter_dimension=0, tiled=...  91.1 us
    all_gather x2, waiting for transfers between devices, spread_grads(): return lax.all_gather(values_in, 'tensor', axis=1, tiled=True)  85.8 us
    all_gather x2, waiting for transfers between devices, broadcast_rows(): return lax.all_gather(values_in, 'tensor', axis=1, tiled=True)  66.3 us
    reduce_scatter x1, waiting for transfers between devices, body(): lax.psum_scatter(grad_output_w, ('shard', 'ctx'), scatter_dimension=0, ti...  55.6 us
    reduce_scatter x1, waiting for transfers between devices, body(): lax.psum_scatter(grad_query_w, ('shard', 'ctx'), scatter_dimension=0, til...  55.1 us
  transfers between devices with their start and end apart: 20, of which 19 were waited for; matrix products, arithmetic and copies ran while one was open for 10% of the time, Pallas kernels for 0%

commit v1 on v0

--- a/solution.py
+++ b/solution.py
@@ -62,7 +62,35 @@
 
 
 def spread_grads(values_in):
-    return lax.all_gather(values_in, "tensor", axis=1, tiled=True)
+
+    def produce_paths(slab_in, on_dim):
+        x_now = lax.psum(1, axis_name="tensor")
+        n_now = lax.axis_index("tensor")
+        placed, o_now, r2 = (x_now, n_now, slab_in.shape[on_dim])
+        a_next = map(lambda idx: (idx, (idx + 1) % placed), range(placed))
+        buffer = list(a_next)
+        pages = list(map(lambda idx: (idx, (idx - 1) % placed), range(placed)))
+        out_arr = jnp.zeros(
+            (*slab_in.shape[:on_dim], placed * r2, *slab_in.shape[on_dim + 1 :]), slab_in.dtype
+        )
+        out_arr = lax.dynamic_update_slice_in_dim(out_arr, slab_in, o_now * r2, axis=on_dim)
+        before = outer = slab_in
+        latest = placed // 2
+        hop_no = 1
+        while hop_no < latest + 1:
+            before = lax.ppermute(before, axis_name="tensor", perm=buffer)
+            out_arr = lax.dynamic_update_slice_in_dim(
+                out_arr, before, (o_now - hop_no) % placed * r2, axis=on_dim
+            )
+            if hop_no < placed - latest:
+                outer = lax.ppermute(outer, axis_name="tensor", perm=pages)
+                out_arr = lax.dynamic_update_slice_in_dim(
+                    out_arr, outer, (o_now + hop_no) % placed * r2, axis=on_dim
+                )
+            hop_no = hop_no + 1
+        return out_arr
+
+    return produce_paths(values_in, on_dim=1)
 
 
 def branch_sum(partial_sum):

time: 1330 us -> 1280 us (0.962)
  waiting for transfers between devices: 924 us -> 853 us
  starting transfers between devices: 1.97 us -> 27.1 us
    all_gather x2 -> x0, waiting for transfers between devices: 85.8 us -> none  [spread_grads(): return lax.all_gather(values_in, 'tensor', axis=1, tiled=True)]
    reduce_scatter x1, waiting for transfers between devices: 37.7 us -> 91.1 us  [body(): lax.psum_scatter(grad_down_w, ('shard', 'ctx'), scatter_dimension=0, tile...]
    reduce_scatter x2, waiting for transfers between devices: 153 us -> 105 us  [input_sum(): lax.psum_scatter(partial_sum, 'tensor', scatter_dimension=1, tiled=True)]
    ppermute x0 -> x6, waiting for transfers between devices: none -> 44.1 us  [the longest x4 43.2 us: produce_paths(): before = lax.ppermute(before, axis_name='tensor', perm=buffer)]
    all_gather x1, waiting for transfers between devices: 40.3 us -> 2.85 us  [body(): lax.all_gather(w_up, ('shard', 'ctx'), axis=0, tiled=True)]
    ppermute x0 -> x6, starting transfers between devices: none -> 26.2 us  [the longest x4 21.5 us: produce_paths(): before = lax.ppermute(before, axis_name='tensor', perm=buffer)]
  transfers between devices with their start and end apart: 20 -> 24, of which waited for: 19 -> 23; matrix products, arithmetic and copies ran while one was open for 10% -> 9% of each run, Pallas kernels for 0% -> 0%
where the time goes in v1:
time: 1280 us; the launch traced here: 1270 us
  waiting for transfers between devices  853 us (67%)
  matrix products  197 us (15%)
  blocking collectives  106 us (8%)
  other arithmetic  44.8 us (4%)
  starting transfers between devices  27.1 us (2%)
  local copies, waits for them, and re-layouts  25.2 us (2%)
  between operations  15.6 us (1%)
    reduce_scatter x2, waiting for transfers between devices, input_sum(): lax.psum_scatter(partial_sum, 'tensor', scatter_dimension=1, tiled=True)  105 us
    reduce_scatter x2, waiting for transfers between devices, branch_sum(): lax.psum_scatter(partial_sum, 'tensor', scatter_dimension=1, tiled=True)  101 us
    reduce_scatter x1, waiting for transfers between devices, body(): lax.psum_scatter(grad_gate_w, ('shard', 'ctx'), scatter_dimension=0, tile...  91.1 us
    reduce_scatter x1, waiting for transfers between devices, body(): lax.psum_scatter(grad_down_w, ('shard', 'ctx'), scatter_dimension=0, tile...  91.1 us
    reduce_scatter x1, waiting for transfers between devices, body(): lax.psum_scatter(grad_up_w, ('shard', 'ctx'), scatter_dimension=0, tiled=...  91.1 us
    all_gather x2, waiting for transfers between devices, broadcast_rows(): return lax.all_gather(values_in, 'tensor', axis=1, tiled=True)  66.8 us
    reduce_scatter x1, waiting for transfers between devices, body(): lax.psum_scatter(grad_output_w, ('shard', 'ctx'), scatter_dimension=0, ti...  55.5 us
    reduce_scatter x1, waiting for transfers between devices, body(): lax.psum_scatter(grad_query_w, ('shard', 'ctx'), scatter_dimension=0, til...  55.1 us
  transfers between devices with their start and end apart: 24, of which 23 were waited for; matrix products, arithmetic and copies ran while one was open for 9% of the time, Pallas kernels for 0%

profile of v1, /device:TPU:0, one launch (start us, length us, event | category | flops | bytes accessed | tf_op | source)
XLA Modules:
  0.0 1269.6 jit_solution(16839509110044913879)
XLA Ops:
  7.9 14.8 %all-gather.1 = bf16[8,1,256]{2,1,0:T(2,128)(2,1)S(1)} all-gather(bf16[1,1,256]{2,1,0:T(2,128)(2,1)S(1)} %reshape.788), channel_id=1, replica_groups=mesh['shard'=2,'ctx'=4,'tensor'=4] {'shard','ctx'}, dimensions={0}, use_global_device_ids=true | all-gather | bytes 4608 | tf_op jit(solution)/shard_map/all_gather | solution.py:137
  27.9 26.3 %all_gather.44 = bf16[2048,128]{1,0:T(8,128)(2,1)S(1)} all-gather(bf16[256,128]{1,0:T(8,128)(2,1)S(1)} %copy-done.18), channel_id=1, replica_groups=mesh['shard'=2,'ctx'=4,'tensor'=4] {'shard','ctx'}, dimensions={0}, use_global_device_ids=true | all-gather | bytes 589824 | tf_op jit(solution)/shard_map/all_gather | solution.py:139
  54.5 18.8 %all-gather.11.cloned.1.call-done = bf16[1,512,2048]{2,1,0:T(8,128)(2,1)} async-done(((bf16[1,128,2048]{2,1,0:T(8,128)(2,1)}), bf16[1,512,2048]{2,1,0:T(8,128)(2,1)}) %all-gather.11.cloned.1.call-update) | async-done | bytes 2097168 | tf_op jit(solution)/shard_map/all_gather | solution.py:61
  76.1 12.3 all-gather
  88.6 13.2 %all-gather.13.cloned.1.call-done = bf16[2048,512]{1,0:T(8,128)(2,1)} async-done(((bf16[256,512]{1,0:T(8,128)(2,1)}), bf16[2048,512]{1,0:T(8,128)(2,1)}) %all-gather.13.cloned.1.call-update) | async-done | bytes 2097168 | tf_op jit(solution)/shard_map/all_gather | solution.py:138
  101.8 4.1 copy.42
  105.9 2.9 fusion.50
  110.3 29.6 %while.28 = (s32[]{:T(128)}, bf16[8,1,512,64]{2,3,1,0:T(8,128)(2,1)S(1)}, f32[8,1,512]{2,1,0:T(1,128)S(1)}, bf16[8,1,512,64]{3,2,1,0:T(8,128)(2,1)}, bf16[1,2048...) while((s32[]{:T(128)}, ...), condition=%wide.region_5.6_spmd.clone, body=%wide.region_2.5_spmd.clone.sunk | while | flops 277904896 | bytes 13859421 | solution.py:192
  139.9 5.0 convolution_bitcast_fusion.2
  145.7 13.7 %all-gather.2 = bf16[8,1,256]{2,1,0:T(2,128)(2,1)S(1)} all-gather(bf16[1,1,256]{2,1,0:T(2,128)(2,1)S(1)} %reshape.790), channel_id=1, replica_groups=mesh['shard'=2,'ctx'=4,'tensor'=4] {'shard','ctx'}, dimensions={0}, use_global_device_ids=true | all-gather | bytes 4608 | tf_op jit(solution)/shard_map/all_gather | solution.py:143
  159.4 62.6 %reduce-scatter.12.cloned.1.call-done = f32[1,128,2048]{2,1,0:T(8,128)} async-done(((f32[1,512,2048]{2,1,0:T(8,128)}), f32[1,128,2048]{2,1,0:T(8,128)}) %reduce-scatter.12.cloned.1.call-update) | async-done | bytes 1048592 | tf_op jit(solution)/shard_map/reduce_scatter | solution.py:97
  232.2 10.4 collective-permute-done
  242.6 9.4 collective-permute-start.2
  254.0 10.0 collective-permute-done.2
  267.6 48.0 %all-gather.17.cloned.1.call-done = bf16[1,512,2048]{2,1,0:T(8,128)(2,1)} async-done(((bf16[1,128,2048]{2,1,0:T(8,128)(2,1)}), bf16[1,512,2048]{2,1,0:T(8,128)(2,1)}) %all-gather.17.cloned.1.call-update) | async-done | bytes 2097168 | tf_op jit(solution)/shard_map/all_gather | solution.py:61
  315.7 8.3 fusion.34
  324.0 35.8 %all-gather.19.cloned.1.call-done = bf16[2048,1408]{1,0:T(8,128)(2,1)} async-done(((bf16[256,1408]{1,0:T(8,128)(2,1)}), bf16[2048,1408]{1,0:T(8,128)(2,1)}) %all-gather.19.cloned.1.call-update) | async-done | bytes 5767184 | tf_op jit(solution)/shard_map/all_gather | solution.py:144
  359.8 8.2 fusion.36
  368.0 37.2 %all-gather.23.cloned.1.call-done = bf16[2048,1408]{1,0:T(8,128)(2,1)} async-done(((bf16[256,1408]{1,0:T(8,128)(2,1)}), bf16[2048,1408]{1,0:T(8,128)(2,1)}) %all-gather.23.cloned.1.call-update) | async-done | bytes 5767184 | tf_op jit(solution)/shard_map/all_gather | solution.py:146
  405.2 10.4 multiply_convert_fusion.1
  415.6 3.4 fusion.92
  419.1 7.7 add_bitcast_fusion.1
  426.9 76.9 %reduce-scatter.16.cloned.1.call-done = f32[1,128,2048]{2,1,0:T(8,128)} async-done(((f32[1,512,2048]{2,1,0:T(8,128)}), f32[1,128,2048]{2,1,0:T(8,128)}) %reduce-scatter.16.cloned.1.call-update) | async-done | bytes 1048592 | tf_op jit(solution)/shard_map/reduce_scatter | solution.py:101
  511.2 12.8 %collective-permute-done.3 = bf16[1,128,2048]{2,1,0:T(8,128)(2,1)S(1)} collective-permute-done((bf16[1,128,2048]{2,1,0:T(8,128)(2,1)S(1)}, bf16[1,128,2048]{2,1,0:T(8,128)(2,1)S(1)}, u32[]{:S(2)}, u32[]{:S(2)}) %collective-permute-start.3) | collective-permute-done | bytes 524320 | tf_op jit(solution)/shard_map/ppermute | solution.py:81
  524.1 9.1 collective-permute-start.5
  535.5 10.0 collective-permute-done.5
  546.3 2.9 convolution_convert_fusion
  550.5 96.6 %while.29 = (s32[]{:T(128)}, f32[1,2048,1,128]{1,3,2,0:T(8,128)}, f32[8,1,512,64]{2,3,1,0:T(8,128)}, bf16[8,1,512,64]{3,2,1,0:T(8,128)(2,1)}, bf16[1,2048,1,128]...) while((s32[]{:T(128)}, f32[1,2048,1,128]{1,3,2,0:T(8,128)}, ...), condition=%wide.region_13.14_spmd.clone, body=%wide.region_11.13_spmd.clone.sunk | while | flops 682524160 | bytes 37902968 | solution.py:270
  649.0 3.2 fusion.93
  652.3 21.9 %reduce-scatter.18.cloned.1.call-done = f32[1,512,128]{1,2,0:T(8,128)} async-done(((f32[1,2048,128]{1,2,0:T(8,128)}), f32[1,512,128]{1,2,0:T(8,128)}) %reduce-scatter.18.cloned.1.call-update) | async-done | bytes 262160 | tf_op jit(solution)/shard_map/reduce_scatter | solution.py:273
  676.3 4.9 add_bitcast_fusion
  682.5 7.6 convolution_bitcast_fusion.1
  693.6 4.8 fusion.94
  698.7 3.4 fusion.40
  703.7 7.5 fusion.32
  711.3 7.6 fusion.30
  720.2 8.0 fusion.95
  730.1 28.1 %reduce-scatter.20.cloned.1.call-done = f32[1,128,2048]{2,1,0:T(8,128)} async-done(((f32[1,512,2048]{2,1,0:T(8,128)}), f32[1,128,2048]{2,1,0:T(8,128)}) %reduce-scatter.20.cloned.1.call-update) | async-done | bytes 1048592 | tf_op jit(solution)/shard_map/reduce_scatter | solution.py:101
  759.8 26.9 %all-reduce.2 = (f32[2048]{0:T(1024)S(1)}, f32[2048]{0:T(1024)S(1)}) all-reduce(f32[2048]{0:T(1024)S(1)} %get-tuple-element.244, f32[2048]{0:T(1024)S(1)} %get-tuple-element.242), channel_id=8, replica_groups=mesh['shard'=2,'ctx'=4,'tensor'=4] {'shard','ctx'}, use_global_device_ids=true, to_apply=%region_18.19.clone | all-reduce | flops 4096 | bytes 32768
  786.8 12.4 all-reduce.3
  799.1 38.7 %reduce-scatter.14.cloned.1.call-done = f32[1,128,2048]{2,1,0:T(8,128)} async-done(((f32[1,512,2048]{2,1,0:T(8,128)}), f32[1,128,2048]{2,1,0:T(8,128)}) %reduce-scatter.14.cloned.1.call-update) | async-done | bytes 1048592 | tf_op jit(solution)/shard_map/reduce_scatter | solution.py:97
  837.8 3.2 fusion.60
  841.0 37.5 %reduce-scatter.24.cloned.1.call-done = f32[256,128]{1,0:T(8,128)} async-done(((f32[2048,128]{1,0:T(8,128)}), f32[256,128]{1,0:T(8,128)}) %reduce-scatter.24.cloned.1.call-update) | async-done | bytes 131088 | tf_op jit(solution)/shard_map/reduce_scatter | solution.py:308
  878.5 55.5 %reduce-scatter.26.cloned.1.call-done = f32[256,512]{1,0:T(8,128)} async-done(((f32[2048,512]{1,0:T(8,128)}), f32[256,512]{1,0:T(8,128)}) %reduce-scatter.26.cloned.1.call-update) | async-done | bytes 524304 | tf_op jit(solution)/shard_map/reduce_scatter | solution.py:309
  934.0 55.1 %reduce-scatter.22.cloned.1.call-done = f32[256,512]{1,0:T(8,128)} async-done(((f32[2048,512]{1,0:T(8,128)}), f32[256,512]{1,0:T(8,128)}) %reduce-scatter.22.cloned.1.call-update) | async-done | bytes 524304 | tf_op jit(solution)/shard_map/reduce_scatter | solution.py:307
  989.1 91.1 %reduce-scatter.28.cloned.1.call-done = f32[256,1408]{1,0:T(8,128)} async-done(((f32[2048,1408]{1,0:T(8,128)}), f32[256,1408]{1,0:T(8,128)}) %reduce-scatter.28.cloned.1.call-update) | async-done | bytes 1441808 | tf_op jit(solution)/shard_map/reduce_scatter | solution.py:315
  1080.3 91.1 %reduce-scatter.30.cloned.1.call-done = f32[256,1408]{1,0:T(8,128)} async-done(((f32[2048,1408]{1,0:T(8,128)}), f32[256,1408]{1,0:T(8,128)}) %reduce-scatter.30.cloned.1.call-update) | async-done | bytes 1441808 | tf_op jit(solution)/shard_map/reduce_scatter | solution.py:316
  1171.4 91.1 %reduce-scatter.32.cloned.1.call-done = f32[256,1408]{1,0:T(8,128)} async-done(((f32[2048,1408]{1,0:T(8,128)}), f32[256,1408]{1,0:T(8,128)}) %reduce-scatter.32.cloned.1.call-update) | async-done | bytes 1441808 | tf_op jit(solution)/shard_map/reduce_scatter | solution.py:317
  (270 shorter events, 179.8 us)
Async XLA Ops:
  7.2 20.5 %copy-start.25 = (s32[1,8]{1,0:T(1,128)S(1)}, s32[1,8]{1,0:T(1,128)}, u32[]{:S(2)}) copy-start(s32[1,8]{1,0:T(1,128)} %param.17) | copy-start | bytes 100
  7.2 20.7 %copy-start.18 = (bf16[256,128]{1,0:T(8,128)(2,1)S(1)}, bf16[256,128]{1,0:T(8,128)(2,1)}, u32[]{:S(2)}) copy-start(bf16[256,128]{1,0:T(8,128)(2,1)} %param.20) | copy-start | bytes 196612
  7.2 66.1 %all-gather.11.cloned.1.call-start = ((), (), s32[]{:S(2)}) async-start(), calls=%async_computation.11 | async-start | bytes 2621440 | tf_op jit(solution)/shard_map/all_gather | solution.py:61
  22.7 5.1 copy-start.16
  24.0 3.9 copy-start.21
  26.0 75.7 %all-gather.13.cloned.1.call-start = ((), (), s32[]{:S(2)}) async-start(), calls=%async_computation.12 | async-start | bytes 2359296 | tf_op jit(solution)/shard_map/all_gather | solution.py:138
  26.8 113.1 %all-gather.15.cloned.1.call-start = ((), (), s32[]{:S(2)}) async-start(), calls=%async_computation.13 | async-start | bytes 2359296 | tf_op jit(solution)/shard_map/all_gather | solution.py:140
  27.5 194.4 %reduce-scatter.12.cloned.1.call-start = ((), (), s32[]{:S(2)}) async-start(), calls=%async_computation.14 | async-start | bytes 5242880 | tf_op jit(solution)/shard_map/reduce_scatter | solution.py:97
  27.6 48.4 %copy-start.23 = (f32[32]{0:T(128)}, f32[32]{0:T(128)S(1)}, u32[]{:S(2)}) copy-start(f32[32]{0:T(128)S(1)} %multiply_power_fusion) | copy-start | bytes 388
  27.9 48.2 %copy-start.19 = (f32[1,512]{1,0:T(1,128)}, f32[1,512]{1,0:T(1,128)S(1)}, u32[]{:S(2)}) copy-start(f32[1,512]{1,0:T(1,128)S(1)} %fusion.86) | copy-start | bytes 6148
  54.2 21.9 %copy-start.10 = (bf16[2048,128]{1,0:T(8,128)(2,1)}, bf16[2048,128]{1,0:T(8,128)(2,1)S(1)}, u32[]{:S(2)}) copy-start(bf16[2048,128]{1,0:T(8,128)(2,1)S(1)} %all_gather.44) | copy-start | bytes 1572868
  101.8 4.1 copy-start
  139.9 5.1 copy-start.14
  145.0 77.0 %copy-start.4 = (bf16[1,128,2048]{2,1,0:T(8,128)(2,1)S(1)}, bf16[1,128,2048]{2,1,0:T(8,128)(2,1)}, u32[]{:S(2)}) copy-start(bf16[1,128,2048]{2,1,0:T(8,128)(2,1)} %param.15) | copy-start | bytes 1572868
  145.0 122.6 %all-gather.21.cloned.1.call-start = ((), (), s32[]{:S(2)}) async-start(), calls=%async_computation.17 | async-start | bytes 6488064 | tf_op jit(solution)/shard_map/all_gather | solution.py:145
  145.6 170.1 %all-gather.17.cloned.1.call-start = ((), (), s32[]{:S(2)}) async-start(), calls=%async_computation.15 | async-start | bytes 2621440 | tf_op jit(solution)/shard_map/all_gather | solution.py:61
  223.4 282.3 %copy-start.2 = (f32[1,128,2048]{2,1,0:T(8,128)}, f32[1,128,2048]{2,1,0:T(8,128)S(1)}, u32[]{:S(2)}) copy-start(f32[1,128,2048]{2,1,0:T(8,128)S(1)} %get-tuple-element.285) | copy-start | bytes 3145732
  224.4 135.4 %all-gather.19.cloned.1.call-start = ((), (), s32[]{:S(2)}) async-start(), calls=%async_computation.16 | async-start | bytes 6488064 | tf_op jit(solution)/shard_map/all_gather | solution.py:144
  225.1 180.1 %all-gather.23.cloned.1.call-start = ((), (), s32[]{:S(2)}) async-start(), calls=%async_computation.18 | async-start | bytes 6488064 | tf_op jit(solution)/shard_map/all_gather | solution.py:146
  225.9 277.9 %reduce-scatter.16.cloned.1.call-start = ((), (), s32[]{:S(2)}) async-start(), calls=%async_computation.20 | async-start | bytes 5242880 | tf_op jit(solution)/shard_map/reduce_scatter | solution.py:101
  225.9 16.7 %collective-permute-start = (bf16[1,128,2048]{2,1,0:T(8,128)(2,1)S(1)}, bf16[1,128,2048]{2,1,0:T(8,128)(2,1)S(1)}, u32[]{:S(2)}, u32[]{:S(2)}) collective-permute-start(bf16[1,128,2048]{2,1,0:T(8,128)(2,1)S(1)} %copy-done.12), channel_id=1, source_target_pairs={{0,1},{1,2},{2,3},{3,0},{4,5},{5,6},{6,7},{7,4},{8,9},{9,10},{10,1... | collective-permute-start | bytes 1572872 | tf_op jit(solution)/shard_map/ppermute | solution.py:81
  227.5 25.7 %collective-permute-start.1 = (bf16[1,128,2048]{2,1,0:T(8,128)(2,1)S(1)}, bf16[1,128,2048]{2,1,0:T(8,128)(2,1)S(1)}, u32[]{:S(2)}, u32[]{:S(2)}) collective-permute-start(bf16[1,128,2048]{2,1,0:T(8,128)(2,1)S(1)} %copy-done.12), channel_id=1, source_target_pairs={{0,3},{1,0},{2,1},{3,2},{4,7},{5,4},{6,5},{7,6},{8,11},{9,8},{10,9... | collective-permute-start | bytes 1572872 | tf_op jit(solution)/shard_map/ppermute | solution.py:86
  242.6 21.4 %collective-permute-start.2 = (bf16[1,128,2048]{2,1,0:T(8,128)(2,1)S(1)}, bf16[1,128,2048]{2,1,0:T(8,128)(2,1)S(1)}, u32[]{:S(2)}, u32[]{:S(2)}) collective-permute-start(bf16[1,128,2048]{2,1,0:T(8,128)(2,1)S(1)} %collective-permute-done), channel_id=1, source_target_pairs={{0,1},{1,2},{2,3},{3,0},{4,5},{5,6},{6,7},{7,4},{8,9},{9,10},{10,1... | collective-permute-start | bytes 1572872 | tf_op jit(solution)/shard_map/ppermute | solution.py:81
  405.2 10.4 copy-start.26
  415.6 3.5 copy-start.34
  415.6 3.5 copy-start.33
  426.8 247.4 %reduce-scatter.18.cloned.1.call-start = ((), (), s32[]{:S(2)}) async-start(), calls=%async_computation.21 | async-start | bytes 1310720 | tf_op jit(solution)/shard_map/reduce_scatter | solution.py:273
  507.4 16.7 %collective-permute-start.3 = (bf16[1,128,2048]{2,1,0:T(8,128)(2,1)S(1)}, bf16[1,128,2048]{2,1,0:T(8,128)(2,1)S(1)}, u32[]{:S(2)}, u32[]{:S(2)}) collective-permute-start(bf16[1,128,2048]{2,1,0:T(8,128)(2,1)S(1)} %get-tuple-element.283), channel_id=1, source_target_pairs={{0,1},{1,2},{2,3},{3,0},{4,5},{5,6},{6,7},{7,4},{8,9},{9,10},{10,1... | collective-permute-start | bytes 1572872 | tf_op jit(solution)/shard_map/ppermute | solution.py:81
  508.9 25.7 %collective-permute-start.4 = (bf16[1,128,2048]{2,1,0:T(8,128)(2,1)S(1)}, bf16[1,128,2048]{2,1,0:T(8,128)(2,1)S(1)}, u32[]{:S(2)}, u32[]{:S(2)}) collective-permute-start(bf16[1,128,2048]{2,1,0:T(8,128)(2,1)S(1)} %get-tuple-element.283), channel_id=1, source_target_pairs={{0,3},{1,0},{2,1},{3,2},{4,7},{5,4},{6,5},{7,6},{8,11},{9,8},{10,9... | collective-permute-start | bytes 1572872 | tf_op jit(solution)/shard_map/ppermute | solution.py:86
  511.2 35.0 %copy-start.28 = (bf16[2048,512]{1,0:T(8,128)(2,1)S(1)}, bf16[2048,512]{1,0:T(8,128)(2,1)}, u32[]{:S(2)}) copy-start(bf16[2048,512]{1,0:T(8,128)(2,1)} %all-gather.15.cloned.1.call-done) | copy-start | bytes 6291460
  524.1 21.4 %collective-permute-start.5 = (bf16[1,128,2048]{2,1,0:T(8,128)(2,1)S(1)}, bf16[1,128,2048]{2,1,0:T(8,128)(2,1)S(1)}, u32[]{:S(2)}, u32[]{:S(2)}) collective-permute-start(bf16[1,128,2048]{2,1,0:T(8,128)(2,1)S(1)} %collective-permute-done.3), channel_id=1, source_target_pairs={{0,1},{1,2},{2,3},{3,0},{4,5},{5,6},{6,7},{7,4},{8,9},{9,10},{10,1... | collective-permute-start | bytes 1572872 | tf_op jit(solution)/shard_map/ppermute | solution.py:81
  647.1 111.0 %reduce-scatter.20.cloned.1.call-start = ((), (), s32[]{:S(2)}) async-start(), calls=%async_computation.22 | async-start | bytes 5242880 | tf_op jit(solution)/shard_map/reduce_scatter | solution.py:101
  649.0 25.2 %copy-start.20 = (f32[1,512]{1,0:T(1,128)S(1)}, f32[1,512]{1,0:T(1,128)}, u32[]{:S(2)}) copy-start(f32[1,512]{1,0:T(1,128)} %copy-done.19) | copy-start | bytes 6148
  649.0 25.2 %copy-start.24 = (f32[32]{0:T(128)S(1)}, f32[32]{0:T(128)}, u32[]{:S(2)}) copy-start(f32[32]{0:T(128)} %copy-done.23) | copy-start | bytes 388
  649.0 27.3 %copy-start.11 = (bf16[2048,128]{1,0:T(8,128)(2,1)S(1)}, bf16[2048,128]{1,0:T(8,128)(2,1)}, u32[]{:S(2)}) copy-start(bf16[2048,128]{1,0:T(8,128)(2,1)} %copy-done.10) | copy-start | bytes 1572868
  681.2 156.6 %reduce-scatter.14.cloned.1.call-start = ((), (), s32[]{:S(2)}) async-start(), calls=%async_computation.19 | async-start | bytes 5242880 | tf_op jit(solution)/shard_map/reduce_scatter | solution.py:97
  690.2 188.3 %reduce-scatter.24.cloned.1.call-start = ((), (), s32[]{:S(2)}) async-start(), calls=%async_computation.24 | async-start | bytes 1179648 | tf_op jit(solution)/shard_map/reduce_scatter | solution.py:308
  693.5 240.5 %reduce-scatter.26.cloned.1.call-start = ((), (), s32[]{:S(2)}) async-start(), calls=%async_computation.25 | async-start | bytes 4718592 | tf_op jit(solution)/shard_map/reduce_scatter | solution.py:309
  698.4 290.7 %reduce-scatter.22.cloned.1.call-start = ((), (), s32[]{:S(2)}) async-start(), calls=%async_computation.23 | async-start | bytes 4718592 | tf_op jit(solution)/shard_map/reduce_scatter | solution.py:307
  702.1 378.2 %reduce-scatter.28.cloned.1.call-start = ((), (), s32[]{:S(2)}) async-start(), calls=%async_computation.26 | async-start | bytes 12976128 | tf_op jit(solution)/shard_map/reduce_scatter | solution.py:315
  711.2 460.1 %reduce-scatter.30.cloned.1.call-start = ((), (), s32[]{:S(2)}) async-start(), calls=%async_computation.27 | async-start | bytes 12976128 | tf_op jit(solution)/shard_map/reduce_scatter | solution.py:316
  718.9 543.6 %reduce-scatter.32.cloned.1.call-start = ((), (), s32[]{:S(2)}) async-start(), calls=%async_computation.28 | async-start | bytes 12976128 | tf_op jit(solution)/shard_map/reduce_scatter | solution.py:317
  728.2 29.9 %copy-start.5 = (bf16[1,128,2048]{2,1,0:T(8,128)(2,1)S(1)}, bf16[1,128,2048]{2,1,0:T(8,128)(2,1)}, u32[]{:S(2)}) copy-start(bf16[1,128,2048]{2,1,0:T(8,128)(2,1)} %param.15) | copy-start | bytes 1572868
  728.2 29.9 %copy-start.17 = (f32[8,1,256]{2,1,0:T(1,128)S(1)}, f32[8,1,256]{2,1,0:T(1,128)}, u32[]{:S(2)}) copy-start(f32[8,1,256]{2,1,0:T(1,128)} %copy-done.16) | copy-start | bytes 24580
  728.2 29.9 %copy-start.22 = (f32[128]{0:T(128)S(1)}, f32[128]{0:T(128)}, u32[]{:S(2)}) copy-start(f32[128]{0:T(128)} %copy-done.21) | copy-start | bytes 1540
  728.2 109.6 %copy-start.8 = (f32[1,128,2048]{2,1,0:T(8,128)S(1)}, f32[1,128,2048]{2,1,0:T(8,128)}, u32[]{:S(2)}) copy-start(f32[1,128,2048]{2,1,0:T(8,128)} %reduce-scatter.16.cloned.1.call-done) | copy-start | bytes 3145732
  728.2 109.6 %copy-start.13 = (bf16[1,128,2048]{2,1,0:T(8,128)(2,1)S(1)}, bf16[1,128,2048]{2,1,0:T(8,128)(2,1)}, u32[]{:S(2)}) copy-start(bf16[1,128,2048]{2,1,0:T(8,128)(2,1)} %param.16) | copy-start | bytes 1572868
  728.3 109.6 %copy-start.3 = (f32[1,128,2048]{2,1,0:T(8,128)S(1)}, f32[1,128,2048]{2,1,0:T(8,128)}, u32[]{:S(2)}) copy-start(f32[1,128,2048]{2,1,0:T(8,128)} %copy-done.2) | copy-start | bytes 3145732
  (11 other events, 18.4 us)
Sparse Core Ops, SparseCore 0:
  26.2 47.0 all-gather.10
  75.1 26.5 all-gather.12
  103.7 27.8 all-gather.14
  145.1 76.7 reduce-scatter.11
  223.8 43.7 all-gather.20
  269.7 45.9 all-gather.16
  317.7 42.0 all-gather.18
  361.8 43.3 all-gather.22
  426.9 76.7 reduce-scatter.15
  647.3 26.8 reduce-scatter.17
  681.3 76.7 reduce-scatter.19
  760.3 77.4 reduce-scatter.13
  841.9 36.5 reduce-scatter.23
  882.6 51.3 reduce-scatter.25
  937.8 51.2 reduce-scatter.21
  993.4 86.7 reduce-scatter.27
  1084.6 86.7 reduce-scatter.29
  1175.7 86.7 reduce-scatter.31
